TPU v7x, 32 devices: a whole 2x2x4 slice. The times are simulated.
32 devices in a mesh: members: 2 (over y), lat: 4 (over z), lev: 2 (over x), sub: 2 (over core).
Axes of the slice: x: 2, y: 2, z: 4, core: 2. Of those that a mesh axis runs over, the one named last changes fastest.
Arguments:
- thermal_state_grid: bfloat16 [272, 512, 1024], P(('members', 'lev', 'sub'), 'lat'), parts along dimension 0, may hold values from -6 to 6
- thermal_forcing: bfloat16 [272, 512, 1024], P(('members', 'lev', 'sub'), 'lat'), parts along dimension 0, may hold values from -6 to 6
- spherical_basis_table: bfloat16 [512, 512, 512], P(('lat', 'lev', 'sub')), may hold values from -0.25 to 0.25
- implicit_solver_matrix: bfloat16 [512, 136, 136], P(('lat', 'lev', 'sub')), may hold values from -0.5 to 0.5
- fourier_order_holder: int32 [512], replicated, may hold values from 0 to 511, as said below
Outputs:
- new_temperature: bfloat16 [272, 512, 1024], P(('members', 'lev', 'sub'), 'lat'), parts along dimension 0
There are 2 independent parts, one for each index of `members`. A program takes and returns all parts, laid end to end along the dimension named above; an argument that names none is the same for every part. Nothing has to cross between parts.
Inputs may be any that keep to these rules, and one draw needn't show every extreme that they name: fourier_order_holder is a permutation of the waves; slots 2k and 2k+1 hold waves m and 511-m for some m.
All inputs are finite; a program needn't handle non-finite values.
Results may differ from a plain program's by a relative error of at most 0.0079.
Values may be sent and summed in bfloat16 or wider, within the bound.
A program may use at most 192 MiB of HBM per device.

v0:
```python
import math
import jax
import jax.numpy as jnp
from jax import lax
from jax.sharding import PartitionSpec as P


def raw_table(fourier_order_holder, lon_count):
    meridian_position = jnp.arange(lon_count, dtype=jnp.int32)
    phases = meridian_position[:, None] * fourier_order_holder[None, :] % lon_count
    angles = phases.astype(jnp.float32) * (2.0 * math.pi / lon_count)
    factor = 1.0 / math.sqrt(lon_count)
    stacked = jnp.stack([jnp.cos(angles), -jnp.sin(angles)], axis=2)
    return stacked.reshape(lon_count, 2 * fourier_order_holder.shape[0]) * factor


def shards(
    thermal_state_grid,
    thermal_forcing,
    spherical_basis_table,
    implicit_solver_matrix,
    fourier_order_holder,
):
    layer_group_span, parallel_group_span, meridian_position = thermal_state_grid.shape
    slot_count, lat_total, wave_total = spherical_basis_table.shape
    present_state = thermal_state_grid.astype(jnp.float32)
    explicit = (
        present_state
        + 0.5 * thermal_forcing.astype(jnp.float32)
        - 0.3
        * present_state
        * present_state
        * present_state
        / (1.0 + present_state * present_state)
    ).astype(jnp.bfloat16)
    raw = raw_table(fourier_order_holder, meridian_position)
    analysis = raw.astype(jnp.bfloat16)
    weights = jnp.where(fourier_order_holder == 0, 1.0, 2.0).astype(jnp.float32)
    synthesis = (raw.T * jnp.repeat(weights, 2)[:, None]).astype(jnp.bfloat16)
    spectral = jnp.dot(
        explicit.reshape(layer_group_span * parallel_group_span, meridian_position),
        analysis,
        preferred_element_type=jnp.float32,
    )
    spectral = spectral.astype(jnp.bfloat16).reshape(
        layer_group_span, parallel_group_span, meridian_position
    )
    banded = lax.all_to_all(spectral, "lat", split_axis=2, concat_axis=1, tiled=True)
    gathered = lax.all_gather(spherical_basis_table, ("lev", "sub"), axis=0, tiled=True)
    owner_slots = gathered.shape[0]
    by_slot = banded.reshape(layer_group_span, lat_total, owner_slots, 2)
    part_spec = jnp.einsum(
        "lxsc,sxn->lscn", by_slot, gathered, preferred_element_type=jnp.float32
    ).astype(jnp.bfloat16)
    column = lax.all_to_all(part_spec, ("lev", "sub"), split_axis=1, concat_axis=0, tiled=True)
    solved = jnp.einsum(
        "skl,lscn->kscn", implicit_solver_matrix, column, preferred_element_type=jnp.float32
    )
    owner_index = lax.axis_index(("lat", "lev", "sub"))
    my_waves = lax.dynamic_slice_in_dim(fourier_order_holder, owner_index * slot_count, slot_count)
    degrees = jnp.arange(wave_total, dtype=jnp.int32)
    live_mask = degrees[None, :] >= my_waves[:, None]
    solved = jnp.where(live_mask[None, :, None, :], solved, 0.0).astype(jnp.bfloat16)
    returned = lax.all_to_all(solved, ("lev", "sub"), split_axis=0, concat_axis=1, tiled=True)
    synthesized = jnp.einsum(
        "sxn,lscn->lxsc", gathered, returned, preferred_element_type=jnp.float32
    ).astype(jnp.bfloat16)
    synthesized = synthesized.reshape(layer_group_span, lat_total, 2 * owner_slots)
    grid_spec = lax.all_to_all(synthesized, "lat", split_axis=1, concat_axis=2, tiled=True)
    result = jnp.dot(
        grid_spec.reshape(layer_group_span * parallel_group_span, meridian_position),
        synthesis,
        preferred_element_type=jnp.float32,
    )
    return result.astype(jnp.bfloat16).reshape(
        layer_group_span, parallel_group_span, meridian_position
    )


def solution(mesh):
    return jax.shard_map(
        shards,
        mesh=mesh,
        in_specs=(
            P(("members", "lev", "sub"), "lat", None),
            P(("members", "lev", "sub"), "lat", None),
            P(("lat", "lev", "sub"), None, None),
            P(("lat", "lev", "sub"), None, None),
            P(),
        ),
        out_specs=P(("members", "lev", "sub"), "lat", None),
        check_vma=False,
    )
```

profile of v0, /device:TPU:0, one launch (start us, length us, event | category | flops | bytes accessed | tf_op | source)
XLA Modules:
  0.0 1055.7 jit_solution(9948861162757677807)
XLA Ops:
  6.5 0.7 all-gather.2.cloned.1.call-update
  7.4 8.2 fusion.25
  15.6 4.4 maximum_multiply_fusion
  20.0 7.0 copy.51
  27.0 4.5 convert_element_type.68
  31.5 13.7 %fusion.5 = bf16[34,128,1024]{2,1,0:T(8,128)(2,1)S(1)} fusion(bf16[34,128,1024]{2,1,0:T(8,128)(2,1)} %param.5, bf16[34,128,1024]{2,1,0:T(8,128)(2,1)} %param.6), kind=kLoop, calls=%fused_computation.10 | loop fusion | flops 53477376 | bytes 26738688 | tf_op jit(solution)/shard_map/convert_element_type | solution.py:35
  45.2 11.6 %convolution_convert_fusion.1 = bf16[4352,1024]{1,0:T(8,128)(2,1)} fusion(bf16[4352,1024]{1,0:T(8,128)(2,1)S(1)} %bitcast.63, bf16[1024,1024]{0,1:T(8,128)(2,1)S(1)} %copy-done.2), kind=kOutput, calls=%fused_computation.16 | convolution fusion | flops 9131261952 | bytes 19922944 | tf_op jit(solution)/shard_map/dot_general | solution.py:40
  56.8 15.1 %copy.52 = bf16[34,128,1024]{1,0,2:T(8,128)(2,1)} copy(bf16[34,128,1024]{2,1,0:T(8,128)(2,1)} %bitcast.61) | data formatting | bytes 17825792 | tf_op jit(solution)/shard_map/reshape | solution.py:45
  71.9 234.5 %all_to_all.66 = bf16[34,128,1024]{1,0,2:T(8,128)(2,1)S(1)} all-to-all(bf16[34,128,1024]{1,0,2:T(8,128)(2,1)} %copy.52), channel_id=1, replica_groups=mesh['members'=2,'lat'=4,'lev'=2,'sub'=2] {'lat'}, dimensions={2} | all-to-all | bytes 17825792 | tf_op jit(solution)/shard_map/all_to_all | solution.py:48
  306.5 8.5 copy.70
  314.9 16.5 %reshape.153 = bf16[34,512,128,2]{1,0,3,2:T(8,128)(2,1)} reshape(bf16[34,4,128,256]{2,1,0,3:T(4,128)(2,1)} %copy.70) | data formatting | bytes 17825792 | tf_op jit(solution)/shard_map/reshape | solution.py:51
  331.4 73.0 %all-gather.2.cloned.1.call-done = bf16[128,512,512]{2,1,0:T(8,128)(2,1)} async-done(((bf16[32,512,512]{2,1,0:T(8,128)(2,1)}), bf16[128,512,512]{2,1,0:T(8,128)(2,1)}) %all-gather.2.cloned.1.call-update) | async-done | bytes 67108880 | tf_op jit(solution)/shard_map/all_gather | solution.py:49
  404.4 30.4 %convert_bitcast_fusion = bf16[34,128,2,512]{3,0,2,1:T(8,128)(2,1)} fusion(bf16[34,512,128,2]{1,0,3,2:T(8,128)(2,1)} %reshape.153, bf16[128,512,512]{2,1,0:T(8,128)(2,1)} %all-gather.2.cloned.1.call-done), kind=kOutput, calls=%fused_computation.14 | convolution fusion | flops 4567859200 | bytes 84934656 | tf_op jit(solution)/shard_map/lxsc,sxn->lscn/dot_general | solution.py:52
  434.8 13.8 %copy.56 = bf16[34,128,2,512]{3,2,0,1:T(2,128)(2,1)} copy(bf16[34,128,2,512]{3,0,2,1:T(8,128)(2,1)} %convert_bitcast_fusion) | data formatting | bytes 17825792 | tf_op jit(solution)/shard_map/convert_element_type | solution.py:54
  448.6 6.0 all-to-all-start.1
  454.7 98.6 %all-to-all-done.1 = bf16[34,128,2,512]{3,2,0,1:T(2,128)(2,1)} async-done(((bf16[34,128,2,512]{3,2,0,1:T(2,128)(2,1)}), bf16[34,128,2,512]{3,2,0,1:T(2,128)(2,1)}, u32[]{:S(2)}, u32[]{:S(2)}) %all-to-all-start.1) | async-done | bytes 8912928 | tf_op jit(solution)/shard_map/all_to_all | solution.py:55
  553.3 9.5 copy.57
  562.8 8.8 copy.58
  571.6 16.3 %fusion.14 = bf16[136,32,2,512]{3,0,2,1:T(8,128)(2,1)S(1)} fusion(bf16[136,32,2,512]{3,1,2,0:T(8,128)(2,1)} %bitcast.62, pred[32,512]{1,0:T(8,128)(4,1)S(1)} %iota_compare_fusion, bf16[32,136,136]{2,1,0:T(8,128)(2,1)S(1)} %copy-done), kind=kOutput, calls=%fused_computation.19 | convolution fusion | flops 1221066752 | bytes 19025920 | tf_op jit(solution)/shard_map/skl,lscn->kscn/dot_general | solution.py:56
  587.8 11.6 %copy.60 = bf16[136,32,2,512]{3,2,1,0:T(2,128)(2,1)S(1)} copy(bf16[136,32,2,512]{3,0,2,1:T(8,128)(2,1)S(1)} %fusion.14) | data formatting | bytes 17825792 | tf_op jit(solution)/shard_map/convert_element_type | solution.py:63
  599.4 103.0 %all_to_all.67 = bf16[136,32,2,512]{3,2,1,0:T(2,128)(2,1)} all-to-all(bf16[136,32,2,512]{3,2,1,0:T(2,128)(2,1)S(1)} %copy.60), channel_id=1, replica_groups=mesh['members'=2,'lat'=4,'lev'=2,'sub'=2] {'lev','sub'}, dimensions={0} | all-to-all | bytes 17825792 | tf_op jit(solution)/shard_map/all_to_all | solution.py:64
  702.4 9.8 copy.61
  712.2 12.8 %copy.62 = bf16[34,4,32,2,512]{4,0,3,2,1:T(8,128)(2,1)} copy(bf16[34,4,32,2,512]{4,2,3,0,1:T(8,128)(2,1)} %bitcast.58) | data formatting | bytes 17825792 | tf_op jit(solution)/shard_map/all_to_all | solution.py:64
  725.0 33.8 %fusion.11 = bf16[128,34,2,512]{3,1,2,0:T(8,128)(2,1)} fusion(bf16[34,128,2,512]{3,0,2,1:T(8,128)(2,1)} %bitcast.55, bf16[128,512,512]{2,1,0:T(8,128)(2,1)} %all-gather.2.cloned.1.call-done), kind=kOutput, calls=%fused_computation.18 | convolution fusion | flops 4567859200 | bytes 84934656 | tf_op jit(solution)/shard_map/sxn,lscn->lxsc/dot_general | solution.py:65
  758.8 17.4 %copy.63 = bf16[34,512,256]{2,0,1:T(8,128)(2,1)} copy(bf16[34,512,256]{1,0,2:T(8,128)(2,1)} %bitcast.56) | data formatting | bytes 17825792 | tf_op jit(solution)/shard_map/reshape | solution.py:68
  776.2 6.2 all-to-all-start.3
  782.4 7.3 copy.66
  789.7 6.1 mul.115
  796.1 214.2 %all-to-all-done.3 = bf16[34,512,256]{2,0,1:T(8,128)(2,1)} async-done(((bf16[34,512,256]{2,0,1:T(8,128)(2,1)}), bf16[34,512,256]{2,0,1:T(8,128)(2,1)}, u32[]{:S(2)}, u32[]{:S(2)}) %all-to-all-start.3) | async-done | bytes 8912928 | tf_op jit(solution)/shard_map/all_to_all | solution.py:69
  1010.3 12.9 %copy.65 = bf16[34,128,4,256]{3,2,1,0:T(4,128)(2,1)} copy(bf16[34,128,4,256]{3,0,1,2:T(8,128)(2,1)} %bitcast.21) | data formatting | bytes 17825792 | tf_op jit(solution)/shard_map/all_to_all | solution.py:69
  1023.2 9.9 copy.73
  1033.1 15.6 %convolution_convert_fusion = bf16[4352,1024]{1,0:T(8,128)(2,1)} fusion(bf16[4352,1024]{1,0:T(8,128)(2,1)} %bitcast.60, f32[1024,1024]{0,1:T(8,128)} %mul.115, f32[1024]{0:T(1024)S(1)} %mul.116), kind=kOutput, calls=%fused_computation.15 | convolution fusion | flops 9133359104 | bytes 22024192 | tf_op jit(solution)/shard_map/dot_general | solution.py:70
  (14 shorter events, 0.6 us)
Async XLA Ops:
  6.5 565.0 %copy-start = (bf16[32,136,136]{2,1,0:T(8,128)(2,1)S(1)}, bf16[32,136,136]{2,1,0:T(8,128)(2,1)}, u32[]{:S(2)}) copy-start(bf16[32,136,136]{2,1,0:T(8,128)(2,1)} %param.8) | copy-start | bytes 3551236
  6.5 0.8 copy-start.3
  6.5 397.8 %all-gather.2.cloned.1.call-start = ((), (), s32[]{:S(2)}) async-start(), calls=%async_computation.4 | async-start | bytes 83886080 | tf_op jit(solution)/shard_map/all_gather | solution.py:49
  31.5 13.7 %copy-start.2 = (bf16[1024,1024]{0,1:T(8,128)(2,1)S(1)}, bf16[1024,1024]{0,1:T(8,128)(2,1)}, u32[]{:S(2)}) copy-start(bf16[1024,1024]{0,1:T(8,128)(2,1)} %convert_element_type.68) | copy-start | bytes 6291460
  448.6 104.7 %all-to-all-start.1 = ((bf16[34,128,2,512]{3,2,0,1:T(2,128)(2,1)}), bf16[34,128,2,512]{3,2,0,1:T(2,128)(2,1)}, u32[]{:S(2)}, u32[]{:S(2)}) async-start(bf16[34,128,2,512]{3,2,0,1:T(2,128)(2,1)} %copy.56), calls=%async_computation.1 | async-start | bytes 17825792 | tf_op jit(solution)/shard_map/all_to_all | solution.py:55
  776.2 234.1 %all-to-all-start.3 = ((bf16[34,512,256]{2,0,1:T(8,128)(2,1)}), bf16[34,512,256]{2,0,1:T(8,128)(2,1)}, u32[]{:S(2)}, u32[]{:S(2)}) async-start(bf16[34,512,256]{2,0,1:T(8,128)(2,1)} %copy.63), calls=%async_computation.3 | async-start | bytes 20971520 | tf_op jit(solution)/shard_map/all_to_all | solution.py:69
  1033.1 15.6 %copy-start.1 = (bf16[32,136,136]{2,1,0:T(8,128)(2,1)S(1)}, bf16[32,136,136]{2,1,0:T(8,128)(2,1)}, u32[]{:S(2)}) copy-start(bf16[32,136,136]{2,1,0:T(8,128)(2,1)} %param.8) | copy-start | bytes 3551236
Sparse Core Ops, SparseCore 0:
  8.9 395.4 all-gather.1
where the time goes:
time: 1060 us
  waiting for transfers between devices  387 us (37%)
  blocking collectives  337 us (32%)
  local copies, waits for them, and re-layouts  172 us (16%)
  matrix products  108 us (10%)
  other arithmetic  26.4 us (2%)
  between operations  13.7 us (1%)
  starting transfers between devices  12.1 us (1%)
    all_to_all x1, blocking collectives, shards(): lax.all_to_all(spectral, 'lat', split_axis=2, concat_axis=1, tiled=True)  235 us
    all_to_all x1, waiting for transfers between devices, shards(): lax.all_to_all(synthesized, 'lat', split_axis=1, concat_axis=2, tiled=True)  214 us
    all_to_all x1, blocking collectives, shards(): lax.all_to_all(solved, ('lev', 'sub'), split_axis=0, concat_axis=1, tiled...  103 us
    all_to_all x1, waiting for transfers between devices, shards(): lax.all_to_all(part_spec, ('lev', 'sub'), split_axis=1, concat_axis=0, ti...  98.6 us
    all_gather x1, waiting for transfers between devices, shards(): lax.all_gather(spherical_basis_table, ('lev', 'sub'), axis=0, tiled=True)  73 us
    dot_general x1, matrix products, shards(): jnp.einsum('sxn,lscn->lxsc', gathered, returned, preferred_element_type=j...  33.8 us
    dot_general x1, matrix products, shards(): jnp.einsum('lxsc,sxn->lscn', by_slot, gathered, preferred_element_type=jn...  30.4 us
    reshape x2, local copies, waits for them, and re-layouts, shards(): by_slot = banded.reshape(layer_group_span, lat_total, owner_slots, 2)  24.9 us
  transfers between devices with their start and end apart: 3, of which 3 were waited for; matrix products, arithmetic and copies ran while one was open for 10% of the time, Pallas kernels for 0%

commit v1 on v0

--- a/solution.py
+++ b/solution.py
@@ -45,7 +45,15 @@
     spectral = spectral.astype(jnp.bfloat16).reshape(
         layer_group_span, parallel_group_span, meridian_position
     )
-    banded = lax.all_to_all(spectral, "lat", split_axis=2, concat_axis=1, tiled=True)
+    ways, here = (lax.axis_size("lat"), lax.axis_index("lat"))
+    width = spectral.shape[2] // ways
+    turned = jnp.roll(spectral, -here * width, axis=2)
+    got = [lax.slice_in_dim(turned, 0, width, axis=2)]
+    for far in range(1, ways):
+        sent = lax.slice_in_dim(turned, far * width, (far + 1) * width, axis=2)
+        got.append(lax.ppermute(sent, "lat", [(d, (d + far) % ways) for d in range(ways)]))
+    line = jnp.concatenate(got[::-1], axis=1)
+    banded = jnp.roll(line, (here + 1) * got[0].shape[1], axis=1)
     gathered = lax.all_gather(spherical_basis_table, ("lev", "sub"), axis=0, tiled=True)
     owner_slots = gathered.shape[0]
     by_slot = banded.reshape(layer_group_span, lat_total, owner_slots, 2)

time: 1060 us -> 1060 us (level)
  blocking collectives: 337 us -> 103 us
  waiting for transfers between devices: 387 us -> 592 us
  local copies, waits for them, and re-layouts: 172 us -> 185 us
    all_to_all x1 -> x0, blocking collectives: 235 us -> none  [shards(): lax.all_to_all(spectral, 'lat', split_axis=2, concat_axis=1, tiled=True)]
    ppermute x0 -> x3, waiting for transfers between devices: none -> 187 us  [shards(): lax.ppermute(sent, 'lat', [(d, (d + far) % ways) for d in range(ways)])]
    reshape x3 -> x0, local copies, waits for them, and re-layouts: 40 us -> none  [the longest x2 24.9 us: shards(): by_slot = banded.reshape(layer_group_span, lat_total, owner_slots, 2)]
    unnamed x9 -> x20, local copies, waits for them, and re-layouts: 10 us -> 34.7 us
    dynamic_slice x0 -> x2, local copies, waits for them, and re-layouts: none -> 23.6 us  [shards(): banded = jnp.roll(line, (here + 1) * got[0].shape[1], axis=1)]
    all_gather x1, waiting for transfers between devices: 73 us -> 91.6 us  [shards(): lax.all_gather(spherical_basis_table, ('lev', 'sub'), axis=0, tiled=True)]
  transfers between devices with their start and end apart: 3 -> 6, of which waited for: 3 -> 5; matrix products, arithmetic and copies ran while one was open for 10% -> 12% of each run, Pallas kernels for 0% -> 0%
where the time goes in v1:
time: 1060 us
  waiting for transfers between devices  592 us (56%)
  local copies, waits for them, and re-layouts  185 us (17%)
  matrix products  109 us (10%)
  blocking collectives  103 us (10%)
  other arithmetic  34.6 us (3%)
  starting transfers between devices  18.1 us (2%)
  between operations  13.7 us (1%)
    all_to_all x1, waiting for transfers between devices, shards(): lax.all_to_all(synthesized, 'lat', split_axis=1, concat_axis=2, tiled=True)  214 us
    ppermute x3, waiting for transfers between devices, shards(): lax.ppermute(sent, 'lat', [(d, (d + far) % ways) for d in range(ways)])  187 us
    all_to_all x1, blocking collectives, shards(): lax.all_to_all(solved, ('lev', 'sub'), split_axis=0, concat_axis=1, tiled...  103 us
    all_to_all x1, waiting for transfers between devices, shards(): lax.all_to_all(part_spec, ('lev', 'sub'), split_axis=1, concat_axis=0, ti...  98.6 us
    all_gather x1, waiting for transfers between devices, shards(): lax.all_gather(spherical_basis_table, ('lev', 'sub'), axis=0, tiled=True)  91.6 us
    unnamed x20, local copies, waits for them, and re-layouts  34.7 us
    dot_general x1, matrix products, shards(): jnp.einsum('sxn,lscn->lxsc', gathered, returned, preferred_element_type=j...  33.8 us
    dot_general x1, matrix products, shards(): jnp.einsum('lxsc,sxn->lscn', by_slot, gathered, preferred_element_type=jn...  30.4 us
  transfers between devices with their start and end apart: 6, of which 5 were waited for; matrix products, arithmetic and copies ran while one was open for 12% of the time, Pallas kernels for 0%

profile of v1, /device:TPU:0, one launch (start us, length us, event | category | flops | bytes accessed | tf_op | source)
XLA Modules:
  0.0 1055.2 jit_solution(5182452712426769105)
XLA Ops:
  7.4 8.2 fusion.26
  20.0 7.0 copy.36
  27.0 4.6 convert_element_type.68
  31.6 16.7 %fusion.5 = bf16[34,128,1024]{2,1,0:T(8,128)(2,1)} fusion(bf16[34,128,1024]{2,1,0:T(8,128)(2,1)} %param.5, bf16[34,128,1024]{2,1,0:T(8,128)(2,1)} %param.6), kind=kLoop, calls=%fused_computation.10 | loop fusion | flops 53477376 | bytes 26738688 | tf_op jit(solution)/shard_map/convert_element_type | solution.py:35
  48.3 13.4 %convolution_convert_fusion.1 = bf16[4352,1024]{1,0:T(8,128)(2,1)S(1)} fusion(bf16[4352,1024]{1,0:T(8,128)(2,1)} %bitcast.59, bf16[1024,1024]{0,1:T(8,128)(2,1)S(1)} %copy-done.4), kind=kOutput, calls=%fused_computation.18 | convolution fusion | flops 9131261952 | bytes 19922944 | tf_op jit(solution)/shard_map/dot_general | solution.py:40
  61.7 5.2 fusion.8
  73.5 5.2 collective-permute-start
  79.7 48.2 %collective-permute-done = bf16[34,128,256]{2,1,0:T(8,128)(2,1)} collective-permute-done((bf16[34,128,256]{2,1,0:T(8,128)(2,1)}, bf16[34,128,256]{2,1,0:T(8,128)(2,1)}, u32[]{:S(2)}, u32[]{:S(2)}) %collective-permute-start) | collective-permute-done | bytes 2228256 | tf_op jit(solution)/shard_map/ppermute | solution.py:54
  131.2 138.4 %collective-permute-done.1 = bf16[34,128,256]{2,1,0:T(8,128)(2,1)} collective-permute-done((bf16[34,128,256]{2,1,0:T(8,128)(2,1)}, bf16[34,128,256]{2,1,0:T(8,128)(2,1)}, u32[]{:S(2)}, u32[]{:S(2)}) %collective-permute-start.1) | collective-permute-done | bytes 2228256 | tf_op jit(solution)/shard_map/ppermute | solution.py:54
  289.1 8.1 constant_dynamic-slice_fusion
  297.2 15.5 %copy.37 = bf16[34,512,256]{1,0,2:T(8,128)(2,1)} copy(bf16[34,512,256]{2,1,0:T(8,128)(2,1)} %constant_dynamic-slice_fusion) | data formatting | bytes 17825792 | tf_op jit(solution)/shard_map/jit(_roll_dynamic)/dynamic_slice | solution.py:56
  312.8 91.6 %all-gather.2.cloned.1.call-done = bf16[128,512,512]{2,1,0:T(8,128)(2,1)} async-done(((bf16[32,512,512]{2,1,0:T(8,128)(2,1)}), bf16[128,512,512]{2,1,0:T(8,128)(2,1)}) %all-gather.2.cloned.1.call-update) | async-done | bytes 67108880 | tf_op jit(solution)/shard_map/all_gather | solution.py:57
  404.4 30.4 %convert_bitcast_fusion = bf16[34,128,2,512]{3,0,2,1:T(8,128)(2,1)} fusion(bf16[34,512,128,2]{1,0,3,2:T(8,128)(2,1)} %bitcast.50, bf16[128,512,512]{2,1,0:T(8,128)(2,1)} %all-gather.2.cloned.1.call-done), kind=kOutput, calls=%fused_computation.16 | convolution fusion | flops 4567859200 | bytes 84934656 | tf_op jit(solution)/shard_map/lxsc,sxn->lscn/dot_general | solution.py:60
  434.8 13.8 %copy.38 = bf16[34,128,2,512]{3,2,0,1:T(2,128)(2,1)} copy(bf16[34,128,2,512]{3,0,2,1:T(8,128)(2,1)} %convert_bitcast_fusion) | data formatting | bytes 17825792 | tf_op jit(solution)/shard_map/convert_element_type | solution.py:62
  448.6 5.7 all-to-all-start
  454.5 98.6 %all-to-all-done = bf16[34,128,2,512]{3,2,0,1:T(2,128)(2,1)} async-done(((bf16[34,128,2,512]{3,2,0,1:T(2,128)(2,1)}), bf16[34,128,2,512]{3,2,0,1:T(2,128)(2,1)}, u32[]{:S(2)}, u32[]{:S(2)}) %all-to-all-start) | async-done | bytes 8912928 | tf_op jit(solution)/shard_map/all_to_all | solution.py:63
  553.1 9.5 copy.39
  562.6 8.8 copy.40
  571.4 16.3 %fusion.15 = bf16[136,32,2,512]{3,0,2,1:T(8,128)(2,1)S(1)} fusion(bf16[136,32,2,512]{3,1,2,0:T(8,128)(2,1)} %bitcast.58, pred[32,512]{1,0:T(8,128)(4,1)S(1)} %iota_compare_fusion, bf16[32,136,136]{2,1,0:T(8,128)(2,1)S(1)} %copy-done), kind=kOutput, calls=%fused_computation.22 | convolution fusion | flops 1221066752 | bytes 19025920 | tf_op jit(solution)/shard_map/skl,lscn->kscn/dot_general | solution.py:64
  587.7 11.6 %copy.42 = bf16[136,32,2,512]{3,2,1,0:T(2,128)(2,1)S(1)} copy(bf16[136,32,2,512]{3,0,2,1:T(8,128)(2,1)S(1)} %fusion.15) | data formatting | bytes 17825792 | tf_op jit(solution)/shard_map/convert_element_type | solution.py:71
  599.3 102.7 %all_to_all.51 = bf16[136,32,2,512]{3,2,1,0:T(2,128)(2,1)} all-to-all(bf16[136,32,2,512]{3,2,1,0:T(2,128)(2,1)S(1)} %copy.42), channel_id=1, replica_groups=mesh['members'=2,'lat'=4,'lev'=2,'sub'=2] {'lev','sub'}, dimensions={0} | all-to-all | bytes 17825792 | tf_op jit(solution)/shard_map/all_to_all | solution.py:72
  702.0 9.8 copy.43
  711.7 12.8 %copy.44 = bf16[34,4,32,2,512]{4,0,3,2,1:T(8,128)(2,1)} copy(bf16[34,4,32,2,512]{4,2,3,0,1:T(8,128)(2,1)} %bitcast.54) | data formatting | bytes 17825792 | tf_op jit(solution)/shard_map/all_to_all | solution.py:72
  724.5 33.8 %fusion.12 = bf16[128,34,2,512]{3,1,2,0:T(8,128)(2,1)} fusion(bf16[34,128,2,512]{3,0,2,1:T(8,128)(2,1)} %bitcast.51, bf16[128,512,512]{2,1,0:T(8,128)(2,1)} %all-gather.2.cloned.1.call-done), kind=kOutput, calls=%fused_computation.21 | convolution fusion | flops 4567859200 | bytes 84934656 | tf_op jit(solution)/shard_map/sxn,lscn->lxsc/dot_general | solution.py:73
  758.3 17.4 %copy.45 = bf16[34,512,256]{2,0,1:T(8,128)(2,1)} copy(bf16[34,512,256]{1,0,2:T(8,128)(2,1)} %bitcast.52) | data formatting | bytes 17825792 | tf_op jit(solution)/shard_map/reshape | solution.py:76
  775.7 6.1 all-to-all-start.2
  781.8 7.3 copy.48
  789.1 6.1 mul.123
  795.5 214.3 %all-to-all-done.2 = bf16[34,512,256]{2,0,1:T(8,128)(2,1)} async-done(((bf16[34,512,256]{2,0,1:T(8,128)(2,1)}), bf16[34,512,256]{2,0,1:T(8,128)(2,1)}, u32[]{:S(2)}, u32[]{:S(2)}) %all-to-all-start.2) | async-done | bytes 8912928 | tf_op jit(solution)/shard_map/all_to_all | solution.py:77
  1009.8 12.9 %copy.47 = bf16[34,128,4,256]{3,2,1,0:T(4,128)(2,1)} copy(bf16[34,128,4,256]{3,0,1,2:T(8,128)(2,1)} %bitcast.19) | data formatting | bytes 17825792 | tf_op jit(solution)/shard_map/all_to_all | solution.py:77
  1022.7 9.9 copy.52
  1032.6 15.5 %convolution_convert_fusion = bf16[4352,1024]{1,0:T(8,128)(2,1)} fusion(bf16[4352,1024]{1,0:T(8,128)(2,1)} %bitcast.57, f32[1024,1024]{0,1:T(8,128)} %mul.123, f32[1024]{0:T(1024)S(1)} %mul.124), kind=kOutput, calls=%fused_computation.17 | convolution fusion | flops 9133359104 | bytes 22024192 | tf_op jit(solution)/shard_map/dot_general | solution.py:78
  (32 shorter events, 36.1 us)
Async XLA Ops:
  6.5 564.9 %copy-start = (bf16[32,136,136]{2,1,0:T(8,128)(2,1)S(1)}, bf16[32,136,136]{2,1,0:T(8,128)(2,1)}, u32[]{:S(2)}) copy-start(bf16[32,136,136]{2,1,0:T(8,128)(2,1)} %param.8) | copy-start | bytes 3551236
  6.5 0.8 copy-start.5
  6.5 397.8 %all-gather.2.cloned.1.call-start = ((), (), s32[]{:S(2)}) async-start(), calls=%async_computation.3 | async-start | bytes 83886080 | tf_op jit(solution)/shard_map/all_gather | solution.py:57
  31.6 16.7 %copy-start.4 = (bf16[1024,1024]{0,1:T(8,128)(2,1)S(1)}, bf16[1024,1024]{0,1:T(8,128)(2,1)}, u32[]{:S(2)}) copy-start(bf16[1024,1024]{0,1:T(8,128)(2,1)} %convert_element_type.68) | copy-start | bytes 6291460
  66.9 3.6 copy-start.2
  73.5 54.4 %collective-permute-start = (bf16[34,128,256]{2,1,0:T(8,128)(2,1)}, bf16[34,128,256]{2,1,0:T(8,128)(2,1)}, u32[]{:S(2)}, u32[]{:S(2)}) collective-permute-start(bf16[34,128,256]{2,1,0:T(8,128)(2,1)} %get-tuple-element.7), channel_id=1, source_target_pairs={{0,12},{4,0},{8,4},{12,8},{1,13},{5,1},{9,5},{13,9},{2,14},{6,2},{... | collective-permute-start | bytes 6684680 | tf_op jit(solution)/shard_map/ppermute | solution.py:54
  78.7 190.9 %collective-permute-start.1 = (bf16[34,128,256]{2,1,0:T(8,128)(2,1)}, bf16[34,128,256]{2,1,0:T(8,128)(2,1)}, u32[]{:S(2)}, u32[]{:S(2)}) collective-permute-start(bf16[34,128,256]{2,1,0:T(8,128)(2,1)} %get-tuple-element.6), channel_id=1, source_target_pairs={{0,8},{4,12},{8,0},{12,4},{1,9},{5,13},{9,1},{13,5},{2,10},{6,14},... | collective-permute-start | bytes 6684680 | tf_op jit(solution)/shard_map/ppermute | solution.py:54
  78.7 194.2 %collective-permute-start.2 = (bf16[34,128,256]{2,1,0:T(8,128)(2,1)}, bf16[34,128,256]{2,1,0:T(8,128)(2,1)}, u32[]{:S(2)}, u32[]{:S(2)}) collective-permute-start(bf16[34,128,256]{2,1,0:T(8,128)(2,1)} %get-tuple-element.5), channel_id=1, source_target_pairs={{0,4},{4,8},{8,12},{12,0},{1,5},{5,9},{9,13},{13,1},{2,6},{6,10},{... | collective-permute-start | bytes 6684680 | tf_op jit(solution)/shard_map/ppermute | solution.py:54
  79.7 196.4 %copy-start.3 = (bf16[34,128,1024]{2,1,0:T(8,128)(2,1)S(1)}, bf16[34,128,1024]{2,1,0:T(8,128)(2,1)}, u32[]{:S(2)}) copy-start(bf16[34,128,1024]{2,1,0:T(8,128)(2,1)} %copy-done.2) | copy-start | bytes 26738692
  448.6 104.5 %all-to-all-start = ((bf16[34,128,2,512]{3,2,0,1:T(2,128)(2,1)}), bf16[34,128,2,512]{3,2,0,1:T(2,128)(2,1)}, u32[]{:S(2)}, u32[]{:S(2)}) async-start(bf16[34,128,2,512]{3,2,0,1:T(2,128)(2,1)} %copy.38), calls=%async_computation | async-start | bytes 17825792 | tf_op jit(solution)/shard_map/all_to_all | solution.py:63
  775.7 234.1 %all-to-all-start.2 = ((bf16[34,512,256]{2,0,1:T(8,128)(2,1)}), bf16[34,512,256]{2,0,1:T(8,128)(2,1)}, u32[]{:S(2)}, u32[]{:S(2)}) async-start(bf16[34,512,256]{2,0,1:T(8,128)(2,1)} %copy.45), calls=%async_computation.2 | async-start | bytes 20971520 | tf_op jit(solution)/shard_map/all_to_all | solution.py:77
  1032.6 15.6 %copy-start.1 = (bf16[32,136,136]{2,1,0:T(8,128)(2,1)S(1)}, bf16[32,136,136]{2,1,0:T(8,128)(2,1)}, u32[]{:S(2)}) copy-start(bf16[32,136,136]{2,1,0:T(8,128)(2,1)} %param.8) | copy-start | bytes 3551236
Sparse Core Ops, SparseCore 0:
  8.9 395.4 all-gather.1
